TPU v7x, 128 devices: a whole 4x4x4 slice. The times are simulated.
128 devices in a mesh: dx: 8 (over z, core), dy: 16 (over x, y).
Axes of the slice: x: 4, y: 4, z: 4, core: 2. Of those that a mesh axis runs over, the one named last changes fastest.
Arguments:
- orbitals: bfloat16 [112, 224, 13, 256], P('dx', 'dy'), may hold values from -6 to 6
- elem_mats: bfloat16 [16, 32, 2, 512, 512], P('dx', 'dy'), as said below
- conn: int32 [16, 32, 2, 512], P('dx', 'dy'), may hold values from 0 to 3374, as said below
Outputs:
- filtered: float32 [112, 224, 13, 256], P('dx', 'dy')
Inputs may be any that keep to these rules, and one draw needn't show every extreme that they name: conn[e1, e2, e3, k] is ((7 (e1 mod 2) + a) (15) + 7 (e2 mod 2) + b) * 15 + 7 e3 + c for a node (a, b, c) of the element, 0 <= a, b, c <= 7, and each of the element's 512 nodes appears exactly once. `elem_mats`: each element's matrix is symmetric.
All inputs are finite; a program needn't handle non-finite values.
Results may differ from a plain program's by a relative error of at most 0.0059.
Values may be sent and summed in bfloat16 or wider, within the bound.
A program may use at most 128 MiB of HBM per device.

v0:
```python
import math
import jax
import jax.numpy as jnp
from jax import lax
from jax.sharding import PartitionSpec as P

filter_center = 1.5
filter_half = 4.0


def shifted(block, axis, distance):
    devices = range(lax.axis_size(axis))
    route = [(i - distance, i) for i in devices if i - distance in devices]
    return lax.ppermute(block, axis, route)


def apply_operator(field, elem_mats, conn):
    bands = field.shape[3]
    padded = jnp.pad(field, ((0, 0), (0, 0), (1, 1), (0, 0)))
    lower_plane = shifted(padded[-1], "dx", 1)
    extended = jnp.concatenate([lower_plane[None], padded], axis=0)
    side_plane = shifted(extended[:, -1], "dy", 1)
    extended = jnp.concatenate([side_plane[:, None], extended], axis=1)
    width = extended.shape[0]
    depth = extended.shape[2]
    flat = extended.reshape(-1, bands)
    nodes = elem_mats.shape[-1]
    count = elem_mats.shape[0] * elem_mats.shape[1] * elem_mats.shape[2]
    links = conn.reshape(-1)
    rows = jnp.take(flat, links, axis=0).reshape(count, nodes, bands)
    product = jnp.einsum(
        "eij,ejb->eib",
        elem_mats.reshape(count, nodes, nodes),
        rows,
        preferred_element_type=jnp.float32,
    )
    summed = (
        jnp.zeros((flat.shape[0], bands), jnp.float32).at[links].add(product.reshape(-1, bands))
    )
    summed = summed.reshape(width, width, depth, bands)
    back_y = shifted(summed[:, 0], "dy", -1)
    summed = summed[:, 1:].at[:, -1].add(back_y)
    back_x = shifted(summed[0], "dx", -1)
    summed = summed[1:].at[-1].add(back_x)
    return summed[:, :, 1:-1]


def gram_of(left, right):
    return jnp.einsum("rb,rc->bc", left, right, precision=lax.Precision.HIGHEST)


def shards(orbitals, elem_mats, conn):
    previous = orbitals.astype(jnp.float32)
    image = apply_operator(orbitals, elem_mats, conn)
    current = (image - filter_center * previous) / filter_half
    for turn in range(2):
        field = current.astype(jnp.bfloat16)
        image = apply_operator(field, elem_mats, conn)
        following = 2.0 * (image - filter_center * current) / filter_half - previous
        previous, current = (current, following)
    bands = current.shape[3]
    columns = current.reshape(-1, bands)
    gram_local = gram_of(columns, columns)
    gram_total = lax.psum(gram_local, ("dx", "dy"))
    lower = jnp.linalg.cholesky(gram_total)
    identity = jnp.eye(bands, dtype=jnp.float32)
    inverse_lower = lax.linalg.triangular_solve(lower, identity, left_side=True, lower=True)
    basis = jnp.einsum("rb,cb->rc", columns, inverse_lower, precision=lax.Precision.HIGHEST)
    scale = math.sqrt(columns.shape[0] * lax.axis_size(("dx", "dy")))
    return (basis * scale).reshape(current.shape)


def solution(mesh):
    in_specs = (
        P("dx", "dy", None, None),
        P("dx", "dy", None, None, None),
        P("dx", "dy", None, None),
    )
    out_specs = P("dx", "dy", None, None)
    return jax.shard_map(shards, mesh=mesh, in_specs=in_specs, out_specs=out_specs, check_vma=False)
```

profile of v0, /device:TPU:1, one launch (start us, length us, event | category | flops | bytes accessed | tf_op | source)
XLA Modules:
  0.0 521.0 jit_solution(5483834711174866498)
XLA Ops:
  8.5 4.9 collective-permute-start
  15.2 3.2 collective-permute-start.1
  21.9 2.6 reshape.312
  24.5 17.0 %gather_fusion = bf16[4096,256]{1,0:T(8,128)(2,1)} fusion(bf16[3375,256]{1,0:T(8,128)(2,1)S(1)} %reshape.312, s32[4096]{0:T(1024)S(1)} %fusion.33), kind=kCustom, calls=%fused_computation.clone | custom fusion | bytes 4210688 | tf_op jit(solution)/shard_map/jit(_take)/gather | solution.py:30
  41.5 2.1 broadcast_select_fusion
  44.3 3.3 convolution_bitcast_fusion.2
  47.6 5.4 %copy.26 = f32[8,512,256]{2,1,0:T(8,128)} copy(f32[8,512,256]{1,2,0:T(8,128)} %convolution_bitcast_fusion.2) | data formatting | bytes 8388608 | tf_op jit(solution)/shard_map/eij,ejb->eib/dot_general | solution.py:31
  53.0 23.7 %scatter_custom_fusion = f32[3375,256]{1,0:T(8,128)S(1)} fusion(s32[4096]{0:T(1024)S(1)} %bitcast.143, f32[4096,256]{1,0:T(8,128)} %bitcast.129, f32[]{:T(128)} %constant.229.clone.1), kind=kCustom, calls=%fused_computation.31 | custom fusion | flops 1048576 | bytes 3456512 | tf_op jit(solution)/shard_map/scatter-add | solution.py:38
  76.7 2.2 reshape.317
  81.6 7.5 %collective-permute-done.2 = f32[15,15,256]{2,1,0:T(8,128)S(1)} collective-permute-done((f32[15,15,256]{2,1,0:T(8,128)S(1)}, f32[15,15,256]{2,1,0:T(8,128)S(1)}, u32[]{:S(2)}, u32[]{:S(2)}) %collective-permute-start.2) | collective-permute-done | bytes 230432 | tf_op jit(solution)/shard_map/ppermute | solution.py:14
  91.6 6.7 %collective-permute-done.3 = f32[14,15,256]{2,1,0:T(8,128)S(1)} collective-permute-done((f32[14,15,256]{2,1,0:T(8,128)S(1)}, f32[14,15,256]{2,1,0:T(8,128)S(1)}, u32[]{:S(2)}, u32[]{:S(2)}) %collective-permute-start.3) | collective-permute-done | bytes 215072 | tf_op jit(solution)/shard_map/ppermute | solution.py:14
  103.8 3.5 collective-permute-start.5
  107.3 2.8 collective-permute-done.5
  111.7 2.6 reshape.320
  114.2 17.0 %gather_fusion.1 = bf16[4096,256]{1,0:T(8,128)(2,1)} fusion(bf16[3375,256]{1,0:T(8,128)(2,1)S(1)} %reshape.320, s32[4096]{0:T(1024)S(1)} %fusion.33), kind=kCustom, calls=%fused_computation.1.clone | custom fusion | bytes 4210688 | tf_op jit(solution)/shard_map/jit(_take)/gather | solution.py:30
  131.3 2.1 broadcast_select_fusion.1
  134.1 3.3 convolution_bitcast_fusion.1
  137.4 5.4 %copy.32 = f32[8,512,256]{2,1,0:T(8,128)} copy(f32[8,512,256]{1,2,0:T(8,128)} %convolution_bitcast_fusion.1) | data formatting | bytes 8388608 | tf_op jit(solution)/shard_map/eij,ejb->eib/dot_general | solution.py:31
  142.8 24.8 %scatter_custom_fusion.1 = f32[3375,256]{1,0:T(8,128)} fusion(s32[4096]{0:T(1024)S(1)} %bitcast.144, f32[4096,256]{1,0:T(8,128)} %bitcast.130, f32[]{:T(128)} %constant.229.clone.1), kind=kCustom, calls=%fused_computation.29 | custom fusion | flops 1048576 | bytes 3456512 | tf_op jit(solution)/shard_map/scatter-add | solution.py:38
  167.6 4.7 reshape.323
  175.0 8.6 %collective-permute-done.6 = f32[15,15,256]{2,1,0:T(8,128)S(1)} collective-permute-done((f32[15,15,256]{2,1,0:T(8,128)S(1)}, f32[15,15,256]{2,1,0:T(8,128)S(1)}, u32[]{:S(2)}, u32[]{:S(2)}) %collective-permute-start.6) | collective-permute-done | bytes 230432 | tf_op jit(solution)/shard_map/ppermute | solution.py:14
  183.7 3.3 collective-permute-start.7
  187.3 4.0 collective-permute-done.7
  196.9 4.3 collective-permute-start.9
  201.2 2.8 collective-permute-done.9
  205.5 2.6 reshape.326
  208.1 17.0 %gather_fusion.2 = bf16[4096,256]{1,0:T(8,128)(2,1)} fusion(bf16[3375,256]{1,0:T(8,128)(2,1)S(1)} %reshape.326, s32[4096]{0:T(1024)S(1)} %fusion.33), kind=kCustom, calls=%fused_computation.2.clone | custom fusion | bytes 4210688 | tf_op jit(solution)/shard_map/jit(_take)/gather | solution.py:30
  225.1 2.1 broadcast_select_fusion.2
  227.9 3.3 convolution_bitcast_fusion
  231.2 5.4 %copy.36 = f32[8,512,256]{2,1,0:T(8,128)} copy(f32[8,512,256]{1,2,0:T(8,128)} %convolution_bitcast_fusion) | data formatting | bytes 8388608 | tf_op jit(solution)/shard_map/eij,ejb->eib/dot_general | solution.py:31
  236.6 23.7 %scatter_custom_fusion.2 = f32[3375,256]{1,0:T(8,128)S(1)} fusion(s32[4096]{0:T(1024)S(1)} %bitcast.145, f32[4096,256]{1,0:T(8,128)} %bitcast.128, f32[]{:T(128)} %constant.229.clone.1), kind=kCustom, calls=%fused_computation.27 | custom fusion | flops 1048576 | bytes 3456512 | tf_op jit(solution)/shard_map/scatter-add | solution.py:38
  260.3 2.2 reshape.329
  265.2 8.6 %collective-permute-done.10 = f32[15,15,256]{2,1,0:T(8,128)S(1)} collective-permute-done((f32[15,15,256]{2,1,0:T(8,128)S(1)}, f32[15,15,256]{2,1,0:T(8,128)S(1)}, u32[]{:S(2)}, u32[]{:S(2)}) %collective-permute-start.10) | collective-permute-done | bytes 230432 | tf_op jit(solution)/shard_map/ppermute | solution.py:14
  273.9 3.3 collective-permute-start.11
  277.6 3.9 collective-permute-done.11
  281.6 2.6 fusion.2
  284.2 6.0 %convolution_bitcast_fusion.3 = f32[256,256]{0,1:T(8,128)} fusion(f32[14,14,13,256]{3,2,1,0:T(8,128)S(1)} %fusion.2), kind=kOutput, calls=%fused_computation.34 | convolution fusion | flops 2003828736 | bytes 2871296 | tf_op jit(solution)/shard_map/rb,rc->bc/dot_general | solution.py:49
  292.1 147.0 %all-reduce.6.cloned.1.call-done = f32[256,256]{0,1:T(8,128)} async-done(((f32[256,256]{0,1:T(8,128)}), f32[256,256]{0,1:T(8,128)}) %all-reduce.6.cloned.1.call-update) | async-done | bytes 262160 | tf_op jit(solution)/shard_map/psum | solution.py:64
  441.1 11.7 %cholesky.50 = f32[128,128]{1,0:T(8,128)S(1)} custom-call(f32[128,128]{1,0:T(8,128)S(1)} %cholesky.118), custom_call_target="Cholesky" | custom-call | tf_op jit(solution)/shard_map/jit(cholesky)/cholesky | solution.py:65
  452.9 10.0 %custom-call.14 = f32[1,128,128]{1,2,0:T(8,128)S(1)} custom-call(f32[1,128,128]{2,1,0:T(8,128)S(1)} %get-tuple-element.99), custom_call_target="InvertDiagBlocksLowerTriangular" | custom-call | tf_op jit(solution)/shard_map/jit(cholesky)/cholesky | solution.py:65
  463.3 11.7 %cholesky.105 = f32[128,128]{1,0:T(8,128)S(1)} custom-call(f32[128,128]{1,0:T(8,128)S(1)} %convolution_subtract_fusion.1), custom_call_target="Cholesky" | custom-call | tf_op jit(solution)/shard_map/jit(cholesky)/cholesky | solution.py:65
  477.3 5.5 %while.7 = (s32[]{:T(128)}, f32[256,256]{1,0:T(8,128)S(1)}, s32[2,2]{1,0:T(2,128)S(1)}, f32[2,128,128]{2,1,0:T(8,128)}, s32[]{:T(128)}) while((s32[]{:T(128)}, f32[256,256]{1,0:T(8,128)S(1)}, s32[2,2]{1,0:T(2,128)S(1)}, f32[2,128,128]{2,1,0:T(8,128)}, s32[]{:T(128)}) %tuple.48), condition=%wide.while_cond.6, body=%wide.while_body.6.sunk | while | flops 2 | bytes 132705 | solution.py:67
  478.0 2.1 bitcast_dynamic-update-slice_fusion.2
  480.7 2.1 bitcast_dynamic-update-slice_fusion.2
  482.8 20.5 %custom-call.15 = f32[2,128,128]{1,2,0:T(8,128)S(1)} custom-call(f32[2,128,128]{2,1,0:T(8,128)} %get-tuple-element.85), custom_call_target="InvertDiagBlocksLowerTriangular" | custom-call | tf_op jit(solution)/shard_map/triangular_solve | solution.py:67
  504.2 3.7 convolution_multiply_fusion
  507.9 2.6 reshape.333
  510.5 3.5 copy.42
  (106 shorter events, 42.1 us)
Async XLA Ops:
  6.5 6.9 %copy-start.14 = (s32[2,2,2,512]{3,2,1,0:T(2,128)S(1)}, s32[2,2,2,512]{3,2,1,0:T(2,128)}, u32[]{:S(2)}) copy-start(s32[2,2,2,512]{3,2,1,0:T(2,128)} %param.19) | copy-start | bytes 49156
  6.5 432.5 %all-reduce.6.cloned.1.call-start = ((), (), s32[]{:S(2)}) async-start(), calls=%async_computation | async-start | bytes 524288 | tf_op jit(solution)/shard_map/psum | solution.py:64
  8.5 6.7 %collective-permute-start = (bf16[14,15,256]{2,1,0:T(8,128)(2,1)S(1)}, bf16[14,15,256]{2,1,0:T(8,128)(2,1)S(1)}, u32[]{:S(2)}, u32[]{:S(2)}) collective-permute-start(bf16[14,15,256]{2,1,0:T(8,128)(2,1)S(1)} %slice_bitcast_fusion.9), channel_id=1, source_target_pairs={{0,16},{16,32},{32,48},{48,64},{64,80},{80,96},{96,112},{1,17},{17... | collective-permute-start | bytes 322568 | tf_op jit(solution)/shard_map/ppermute | solution.py:14
  15.2 5.1 collective-permute-start.1
  41.5 2.8 copy-start.3
  78.9 10.2 %copy-start.10 = (f32[15,15,15,256]{3,2,1,0:T(8,128)S(1)}, f32[15,15,15,256]{3,2,1,0:T(8,128)}, u32[]{:S(2)}) copy-start(f32[15,15,15,256]{3,2,1,0:T(8,128)} %reshape.317) | copy-start | bytes 10368004
  80.0 9.1 %slice-start = ((f32[15,15,15,256]{3,2,1,0:T(8,128)}), f32[15,14,15,256]{3,2,1,0:T(8,128)S(1)}, s32[]{:S(2)}) async-start(f32[15,15,15,256]{3,2,1,0:T(8,128)} %reshape.317), calls=%async_computation.1 | async-start | bytes 6881280 | tf_op jit(solution)/shard_map/slice | solution.py:42
  80.1 9.1 %collective-permute-start.2 = (f32[15,15,256]{2,1,0:T(8,128)S(1)}, f32[15,15,256]{2,1,0:T(8,128)S(1)}, u32[]{:S(2)}, u32[]{:S(2)}) collective-permute-start(f32[15,15,256]{2,1,0:T(8,128)S(1)} %slice_bitcast_fusion.2), channel_id=1, source_target_pairs={{1,0},{2,1},{3,2},{4,3},{5,4},{6,5},{7,6},{8,7},{9,8},{10,9},{11,1... | collective-permute-start | bytes 691208 | tf_op jit(solution)/shard_map/ppermute | solution.py:14
  89.2 9.2 %copy-start.8 = (bf16[14,14,13,256]{3,1,2,0:T(8,128)(2,1)S(1)}, bf16[14,14,13,256]{3,1,2,0:T(8,128)(2,1)}, u32[]{:S(2)}) copy-start(bf16[14,14,13,256]{3,1,2,0:T(8,128)(2,1)} %param.17) | copy-start | bytes 3913732
  89.2 9.1 %collective-permute-start.3 = (f32[14,15,256]{2,1,0:T(8,128)S(1)}, f32[14,15,256]{2,1,0:T(8,128)S(1)}, u32[]{:S(2)}, u32[]{:S(2)}) collective-permute-start(f32[14,15,256]{2,1,0:T(8,128)S(1)} %slice_bitcast_fusion.6), channel_id=1, source_target_pairs={{16,0},{32,16},{48,32},{64,48},{80,64},{96,80},{112,96},{17,1},{33... | collective-permute-start | bytes 645128 | tf_op jit(solution)/shard_map/ppermute | solution.py:14
  98.4 1.7 copy-start
  100.1 3.7 collective-permute-start.4
  103.8 6.4 %collective-permute-start.5 = (bf16[15,15,256]{2,1,0:T(8,128)(2,1)S(1)}, bf16[15,15,256]{2,1,0:T(8,128)(2,1)S(1)}, u32[]{:S(2)}, u32[]{:S(2)}) collective-permute-start(bf16[15,15,256]{2,1,0:T(8,128)(2,1)S(1)} %fusion.26), channel_id=1, source_target_pairs={{0,1},{1,2},{2,3},{3,4},{4,5},{5,6},{6,7},{7,8},{8,9},{9,10},{10,1... | collective-permute-start | bytes 345608 | tf_op jit(solution)/shard_map/ppermute | solution.py:14
  131.3 2.8 copy-start.4
  172.3 11.3 %copy-start.11 = (f32[15,15,15,256]{3,2,1,0:T(8,128)S(1)}, f32[15,15,15,256]{3,2,1,0:T(8,128)}, u32[]{:S(2)}) copy-start(f32[15,15,15,256]{3,2,1,0:T(8,128)} %reshape.323) | copy-start | bytes 10368004
  173.4 10.2 %slice-start.1 = ((f32[15,15,15,256]{3,2,1,0:T(8,128)}), f32[15,14,15,256]{3,2,1,0:T(8,128)S(1)}, s32[]{:S(2)}) async-start(f32[15,15,15,256]{3,2,1,0:T(8,128)} %reshape.323), calls=%async_computation.2 | async-start | bytes 6881280 | tf_op jit(solution)/shard_map/slice | solution.py:42
  173.4 10.2 %collective-permute-start.6 = (f32[15,15,256]{2,1,0:T(8,128)S(1)}, f32[15,15,256]{2,1,0:T(8,128)S(1)}, u32[]{:S(2)}, u32[]{:S(2)}) collective-permute-start(f32[15,15,256]{2,1,0:T(8,128)S(1)} %slice_bitcast_fusion.1), channel_id=1, source_target_pairs={{1,0},{2,1},{3,2},{4,3},{5,4},{6,5},{7,6},{8,7},{9,8},{10,9},{11,1... | collective-permute-start | bytes 691208 | tf_op jit(solution)/shard_map/ppermute | solution.py:14
  183.7 7.7 %copy-start.1 = (f32[14,14,15,256]{3,2,1,0:T(8,128)S(1)}, f32[14,14,15,256]{3,2,1,0:T(8,128)}, u32[]{:S(2)}) copy-start(f32[14,14,15,256]{3,2,1,0:T(8,128)} %copy-done) | copy-start | bytes 9031684
  183.7 7.6 %collective-permute-start.7 = (f32[14,15,256]{2,1,0:T(8,128)S(1)}, f32[14,15,256]{2,1,0:T(8,128)S(1)}, u32[]{:S(2)}, u32[]{:S(2)}) collective-permute-start(f32[14,15,256]{2,1,0:T(8,128)S(1)} %slice_bitcast_fusion.5), channel_id=1, source_target_pairs={{16,0},{32,16},{48,32},{64,48},{80,64},{96,80},{112,96},{17,1},{33... | collective-permute-start | bytes 645128 | tf_op jit(solution)/shard_map/ppermute | solution.py:14
  191.4 1.8 copy-start.6
  193.2 3.7 collective-permute-start.8
  196.9 7.1 %collective-permute-start.9 = (bf16[15,15,256]{2,1,0:T(8,128)(2,1)S(1)}, bf16[15,15,256]{2,1,0:T(8,128)(2,1)S(1)}, u32[]{:S(2)}, u32[]{:S(2)}) collective-permute-start(bf16[15,15,256]{2,1,0:T(8,128)(2,1)S(1)} %fusion.25), channel_id=1, source_target_pairs={{0,1},{1,2},{2,3},{3,4},{4,5},{5,6},{6,7},{7,8},{8,9},{9,10},{10,1... | collective-permute-start | bytes 345608 | tf_op jit(solution)/shard_map/ppermute | solution.py:14
  225.1 2.8 copy-start.5
  262.5 11.3 %copy-start.12 = (f32[15,15,15,256]{3,2,1,0:T(8,128)S(1)}, f32[15,15,15,256]{3,2,1,0:T(8,128)}, u32[]{:S(2)}) copy-start(f32[15,15,15,256]{3,2,1,0:T(8,128)} %reshape.329) | copy-start | bytes 10368004
  263.7 10.2 %slice-start.2 = ((f32[15,15,15,256]{3,2,1,0:T(8,128)}), f32[15,14,15,256]{3,2,1,0:T(8,128)S(1)}, s32[]{:S(2)}) async-start(f32[15,15,15,256]{3,2,1,0:T(8,128)} %reshape.329), calls=%async_computation.3 | async-start | bytes 6881280 | tf_op jit(solution)/shard_map/slice | solution.py:42
  263.7 10.2 %collective-permute-start.10 = (f32[15,15,256]{2,1,0:T(8,128)S(1)}, f32[15,15,256]{2,1,0:T(8,128)S(1)}, u32[]{:S(2)}, u32[]{:S(2)}) collective-permute-start(f32[15,15,256]{2,1,0:T(8,128)S(1)} %slice_bitcast_fusion), channel_id=1, source_target_pairs={{1,0},{2,1},{3,2},{4,3},{5,4},{6,5},{7,6},{8,7},{9,8},{10,9},{11,1... | collective-permute-start | bytes 691208 | tf_op jit(solution)/shard_map/ppermute | solution.py:14
  265.2 16.3 %copy-start.9 = (bf16[14,14,13,256]{3,1,2,0:T(8,128)(2,1)S(1)}, bf16[14,14,13,256]{3,1,2,0:T(8,128)(2,1)}, u32[]{:S(2)}) copy-start(bf16[14,14,13,256]{3,1,2,0:T(8,128)(2,1)} %param.17) | copy-start | bytes 3913732
  273.9 7.7 %copy-start.2 = (f32[14,14,15,256]{3,2,1,0:T(8,128)S(1)}, f32[14,14,15,256]{3,2,1,0:T(8,128)}, u32[]{:S(2)}) copy-start(f32[14,14,15,256]{3,2,1,0:T(8,128)} %copy-done) | copy-start | bytes 9031684
  273.9 7.7 %copy-start.7 = (f32[14,14,15,256]{3,2,1,0:T(8,128)S(1)}, f32[14,14,15,256]{3,2,1,0:T(8,128)}, u32[]{:S(2)}) copy-start(f32[14,14,15,256]{3,2,1,0:T(8,128)} %copy-done.6) | copy-start | bytes 9031684
  273.9 7.6 %collective-permute-start.11 = (f32[14,15,256]{2,1,0:T(8,128)S(1)}, f32[14,15,256]{2,1,0:T(8,128)S(1)}, u32[]{:S(2)}, u32[]{:S(2)}) collective-permute-start(f32[14,15,256]{2,1,0:T(8,128)S(1)} %slice_bitcast_fusion.4), channel_id=1, source_target_pairs={{16,0},{32,16},{48,32},{64,48},{80,64},{96,80},{112,96},{17,1},{33... | collective-permute-start | bytes 645128 | tf_op jit(solution)/shard_map/ppermute | solution.py:14
  292.1 212.1 %copy-start.13 = (f32[2548,256]{1,0:T(8,128)S(1)}, f32[2548,256]{1,0:T(8,128)}, u32[]{:S(2)}) copy-start(f32[2548,256]{1,0:T(8,128)} %reshape.332) | copy-start | bytes 7827460
Sparse Core Ops, SparseCore 0:
  290.3 148.6 all-reduce.5
where the time goes:
time: 530 us; the launch traced here: 521 us
  waiting for transfers between devices  197 us (37%)
  other arithmetic  143 us (27%)
  local copies, waits for them, and re-layouts  111 us (21%)
  starting transfers between devices  33.1 us (6%)
  matrix products  21 us (4%)
  between operations  15.6 us (3%)
    psum x1, waiting for transfers between devices, shards(): gram_total = lax.psum(gram_local, ('dx', 'dy'))  147 us
    scatter-add x3, other arithmetic, apply_operator(): jnp.zeros((flat.shape[0], bands), jnp.float32).at[links]  72.1 us
    gather x3, local copies, waits for them, and re-layouts, apply_operator(): rows = jnp.take(flat, links, axis=0).reshape(count, nodes, bands)  51.1 us
    ppermute x12, waiting for transfers between devices, shifted(): return lax.ppermute(block, axis, route)  50 us
    another operation x6, other arithmetic, shards(): lower = jnp.linalg.cholesky(gram_total)  34.2 us
    ppermute x12, starting transfers between devices, shifted(): return lax.ppermute(block, axis, route)  33.1 us
    another operation x3, other arithmetic, shards(): lax.linalg.triangular_solve(lower, identity, left_side=True, lower=True)  20.5 us
    dot_general x3, local copies, waits for them, and re-layouts, apply_operator(): jnp.einsum('eij,ejb->eib', elem_mats.reshape(count, nodes, nodes), rows,...  16.2 us
  transfers between devices with their start and end apart: 13, of which 13 were waited for; matrix products, arithmetic and copies ran while one was open for 1% of the time, Pallas kernels for 0%

commit v1 on v0

--- a/solution.py
+++ b/solution.py
@@ -61,7 +61,7 @@
     bands = current.shape[3]
     columns = current.reshape(-1, bands)
     gram_local = gram_of(columns, columns)
-    gram_total = lax.psum(gram_local, ("dx", "dy"))
+    gram_total = jnp.sum(lax.all_gather(gram_local, ("dx", "dy")), axis=0)
     lower = jnp.linalg.cholesky(gram_total)
     identity = jnp.eye(bands, dtype=jnp.float32)
     inverse_lower = lax.linalg.triangular_solve(lower, identity, left_side=True, lower=True)

time: 530 us -> 508 us (0.958)
  waiting for transfers between devices: 197 us -> 159 us
  other arithmetic: 143 us -> 155 us
    psum x1 -> x0, waiting for transfers between devices: 147 us -> none  [shards(): gram_total = lax.psum(gram_local, ('dx', 'dy'))]
    all_gather x0 -> x1, waiting for transfers between devices: none -> 110 us  [shards(): gram_total = jnp.sum(lax.all_gather(gram_local, ('dx', 'dy')), axis=0)]
    reduce_sum x0 -> x1, other arithmetic: none -> 12.4 us  [shards(): gram_total = jnp.sum(lax.all_gather(gram_local, ('dx', 'dy')), axis=0)]
where the time goes in v1:
time: 508 us; the launch traced here: 500 us
  waiting for transfers between devices  159 us (31%)
  other arithmetic  155 us (31%)
  local copies, waits for them, and re-layouts  115 us (23%)
  starting transfers between devices  33.3 us (7%)
  matrix products  21.2 us (4%)
  between operations  15.4 us (3%)
    all_gather x1, waiting for transfers between devices, shards(): gram_total = jnp.sum(lax.all_gather(gram_local, ('dx', 'dy')), axis=0)  110 us
    scatter-add x3, other arithmetic, apply_operator(): jnp.zeros((flat.shape[0], bands), jnp.float32).at[links]  73.2 us
    gather x3, local copies, waits for them, and re-layouts, apply_operator(): rows = jnp.take(flat, links, axis=0).reshape(count, nodes, bands)  51.1 us
    ppermute x12, waiting for transfers between devices, shifted(): return lax.ppermute(block, axis, route)  49.8 us
    another operation x6, other arithmetic, shards(): lower = jnp.linalg.cholesky(gram_total)  33.9 us
    ppermute x12, starting transfers between devices, shifted(): return lax.ppermute(block, axis, route)  33.3 us
    another operation x3, other arithmetic, shards(): lax.linalg.triangular_solve(lower, identity, left_side=True, lower=True)  20.7 us
    dot_general x3, local copies, waits for them, and re-layouts, apply_operator(): jnp.einsum('eij,ejb->eib', elem_mats.reshape(count, nodes, nodes), rows,...  16.2 us
  transfers between devices with their start and end apart: 13, of which 13 were waited for; matrix products, arithmetic and copies ran while one was open for 1% of the time, Pallas kernels for 0%

profile of v1, /device:TPU:1, one launch (start us, length us, event | category | flops | bytes accessed | tf_op | source)
XLA Modules:
  0.0 499.6 jit_solution(5677016549311833081)
XLA Ops:
  8.5 4.9 collective-permute-start
  15.2 3.2 collective-permute-start.1
  21.9 2.6 reshape.312
  24.5 17.0 %gather_fusion = bf16[4096,256]{1,0:T(8,128)(2,1)} fusion(bf16[3375,256]{1,0:T(8,128)(2,1)S(1)} %reshape.312, s32[4096]{0:T(1024)S(1)} %fusion.33), kind=kCustom, calls=%fused_computation.clone | custom fusion | bytes 4210688 | tf_op jit(solution)/shard_map/jit(_take)/gather | solution.py:30
  41.5 2.1 broadcast_select_fusion
  44.3 3.3 convolution_bitcast_fusion.2
  47.6 5.4 %copy.45 = f32[8,512,256]{2,1,0:T(8,128)} copy(f32[8,512,256]{1,2,0:T(8,128)} %convolution_bitcast_fusion.2) | data formatting | bytes 8388608 | tf_op jit(solution)/shard_map/eij,ejb->eib/dot_general | solution.py:31
  53.0 23.7 %scatter_custom_fusion = f32[3375,256]{1,0:T(8,128)S(1)} fusion(s32[4096]{0:T(1024)S(1)} %bitcast.147, f32[4096,256]{1,0:T(8,128)} %bitcast.133, f32[]{:T(128)} %constant.230.clone.1), kind=kCustom, calls=%fused_computation.31 | custom fusion | flops 1048576 | bytes 3456512 | tf_op jit(solution)/shard_map/scatter-add | solution.py:38
  76.7 2.2 reshape.317
  81.6 7.5 %collective-permute-done.2 = f32[15,15,256]{2,1,0:T(8,128)S(1)} collective-permute-done((f32[15,15,256]{2,1,0:T(8,128)S(1)}, f32[15,15,256]{2,1,0:T(8,128)S(1)}, u32[]{:S(2)}, u32[]{:S(2)}) %collective-permute-start.2) | collective-permute-done | bytes 230432 | tf_op jit(solution)/shard_map/ppermute | solution.py:14
  91.6 6.7 %collective-permute-done.3 = f32[14,15,256]{2,1,0:T(8,128)S(1)} collective-permute-done((f32[14,15,256]{2,1,0:T(8,128)S(1)}, f32[14,15,256]{2,1,0:T(8,128)S(1)}, u32[]{:S(2)}, u32[]{:S(2)}) %collective-permute-start.3) | collective-permute-done | bytes 215072 | tf_op jit(solution)/shard_map/ppermute | solution.py:14
  103.8 3.5 collective-permute-start.5
  107.4 2.8 collective-permute-done.5
  111.7 2.6 reshape.320
  114.3 17.0 %gather_fusion.1 = bf16[4096,256]{1,0:T(8,128)(2,1)} fusion(bf16[3375,256]{1,0:T(8,128)(2,1)S(1)} %reshape.320, s32[4096]{0:T(1024)S(1)} %fusion.33), kind=kCustom, calls=%fused_computation.1.clone | custom fusion | bytes 4210688 | tf_op jit(solution)/shard_map/jit(_take)/gather | solution.py:30
  131.3 2.1 broadcast_select_fusion.1
  134.1 3.3 convolution_bitcast_fusion.1
  137.5 5.4 %copy.51 = f32[8,512,256]{2,1,0:T(8,128)} copy(f32[8,512,256]{1,2,0:T(8,128)} %convolution_bitcast_fusion.1) | data formatting | bytes 8388608 | tf_op jit(solution)/shard_map/eij,ejb->eib/dot_general | solution.py:31
  142.8 24.8 %scatter_custom_fusion.1 = f32[3375,256]{1,0:T(8,128)} fusion(s32[4096]{0:T(1024)S(1)} %bitcast.148, f32[4096,256]{1,0:T(8,128)} %bitcast.134, f32[]{:T(128)} %constant.230.clone.1), kind=kCustom, calls=%fused_computation.29 | custom fusion | flops 1048576 | bytes 3456512 | tf_op jit(solution)/shard_map/scatter-add | solution.py:38
  167.6 4.7 reshape.323
  175.0 8.6 %collective-permute-done.6 = f32[15,15,256]{2,1,0:T(8,128)S(1)} collective-permute-done((f32[15,15,256]{2,1,0:T(8,128)S(1)}, f32[15,15,256]{2,1,0:T(8,128)S(1)}, u32[]{:S(2)}, u32[]{:S(2)}) %collective-permute-start.6) | collective-permute-done | bytes 230432 | tf_op jit(solution)/shard_map/ppermute | solution.py:14
  183.7 3.3 collective-permute-start.7
  187.3 4.0 collective-permute-done.7
  196.9 4.3 collective-permute-start.9
  201.2 2.8 collective-permute-done.9
  205.5 2.6 reshape.326
  208.1 17.0 %gather_fusion.2 = bf16[4096,256]{1,0:T(8,128)(2,1)} fusion(bf16[3375,256]{1,0:T(8,128)(2,1)S(1)} %reshape.326, s32[4096]{0:T(1024)S(1)} %fusion.33), kind=kCustom, calls=%fused_computation.2.clone | custom fusion | bytes 4210688 | tf_op jit(solution)/shard_map/jit(_take)/gather | solution.py:30
  225.2 2.1 broadcast_select_fusion.2
  228.0 3.3 convolution_bitcast_fusion
  231.3 5.4 %copy.55 = f32[8,512,256]{2,1,0:T(8,128)} copy(f32[8,512,256]{1,2,0:T(8,128)} %convolution_bitcast_fusion) | data formatting | bytes 8388608 | tf_op jit(solution)/shard_map/eij,ejb->eib/dot_general | solution.py:31
  236.7 24.8 %scatter_custom_fusion.2 = f32[3375,256]{1,0:T(8,128)} fusion(s32[4096]{0:T(1024)S(1)} %bitcast.149, f32[4096,256]{1,0:T(8,128)} %bitcast.132, f32[]{:T(128)} %constant.230.clone.1), kind=kCustom, calls=%fused_computation.27 | custom fusion | flops 1048576 | bytes 3456512 | tf_op jit(solution)/shard_map/scatter-add | solution.py:38
  261.4 4.7 reshape.329
  268.9 8.6 %collective-permute-done.10 = f32[15,15,256]{2,1,0:T(8,128)S(1)} collective-permute-done((f32[15,15,256]{2,1,0:T(8,128)S(1)}, f32[15,15,256]{2,1,0:T(8,128)S(1)}, u32[]{:S(2)}, u32[]{:S(2)}) %collective-permute-start.10) | collective-permute-done | bytes 230432 | tf_op jit(solution)/shard_map/ppermute | solution.py:14
  277.6 3.5 collective-permute-start.11
  281.5 3.7 collective-permute-done.11
  285.2 2.4 fusion.2
  289.3 6.2 %convolution_bitcast_fusion.3 = f32[256,256]{1,0:T(8,128)} fusion(f32[14,14,13,256]{3,2,1,0:T(8,128)S(1)} %fusion.2), kind=kOutput, calls=%fused_computation.34 | convolution fusion | flops 2003828736 | bytes 2871296 | tf_op jit(solution)/shard_map/rb,rc->bc/dot_general | solution.py:49
  295.5 2.7 reshape.332
  298.3 109.6 %all-gather.3.cloned.1.call-done = f32[32768,256]{1,0:T(8,128)} async-done(((f32[256,256]{1,0:T(8,128)}), f32[32768,256]{1,0:T(8,128)}) %all-gather.3.cloned.1.call-update) | async-done | bytes 33554448 | tf_op jit(solution)/shard_map/all_gather | solution.py:64
  407.9 12.4 %reduce_sum.9 = f32[256,256]{1,0:T(8,128)S(1)} reduce(f32[128,256,256]{2,1,0:T(8,128)} %bitcast.128, f32[]{:T(128)} %constant.230.clone.1), dimensions={0}, to_apply=%region_3.5 | reduce | flops 8323072 | bytes 33816580 | tf_op jit(solution)/shard_map/reduce_sum | solution.py:64
  420.5 11.7 %cholesky.50 = f32[128,128]{1,0:T(8,128)S(1)} custom-call(f32[128,128]{1,0:T(8,128)S(1)} %cholesky.118), custom_call_target="Cholesky" | custom-call | tf_op jit(solution)/shard_map/jit(cholesky)/cholesky | solution.py:65
  432.3 9.8 %custom-call.14 = f32[1,128,128]{1,2,0:T(8,128)S(1)} custom-call(f32[1,128,128]{2,1,0:T(8,128)S(1)} %get-tuple-element.99), custom_call_target="InvertDiagBlocksLowerTriangular" | custom-call | tf_op jit(solution)/shard_map/jit(cholesky)/cholesky | solution.py:65
  442.6 11.7 %cholesky.105 = f32[128,128]{1,0:T(8,128)S(1)} custom-call(f32[128,128]{1,0:T(8,128)S(1)} %convolution_subtract_fusion.1), custom_call_target="Cholesky" | custom-call | tf_op jit(solution)/shard_map/jit(cholesky)/cholesky | solution.py:65
  456.3 5.0 %while.7 = (s32[]{:T(128)}, f32[256,256]{1,0:T(8,128)S(1)}, s32[2,2]{1,0:T(2,128)S(1)}, f32[2,128,128]{2,1,0:T(8,128)}, s32[]{:T(128)}) while((s32[]{:T(128)}, f32[256,256]{1,0:T(8,128)S(1)}, s32[2,2]{1,0:T(2,128)S(1)}, f32[2,128,128]{2,1,0:T(8,128)}, s32[]{:T(128)}) %tuple.48), condition=%wide.while_cond.6, body=%wide.while_body.6.sunk | while | flops 2 | bytes 132205 | solution.py:67
  461.3 20.6 %custom-call.15 = f32[2,128,128]{1,2,0:T(8,128)S(1)} custom-call(f32[2,128,128]{2,1,0:T(8,128)} %get-tuple-element.85), custom_call_target="InvertDiagBlocksLowerTriangular" | custom-call | tf_op jit(solution)/shard_map/triangular_solve | solution.py:67
  482.8 3.7 convolution_multiply_fusion
  486.5 2.6 reshape.333
  489.1 3.5 copy.58
  (105 shorter events, 43.6 us)
Async XLA Ops:
  6.5 6.9 %copy-start.13 = (s32[2,2,2,512]{3,2,1,0:T(2,128)S(1)}, s32[2,2,2,512]{3,2,1,0:T(2,128)}, u32[]{:S(2)}) copy-start(s32[2,2,2,512]{3,2,1,0:T(2,128)} %param.19) | copy-start | bytes 49156
  6.5 401.4 %all-gather.3.cloned.1.call-start = ((), (), s32[]{:S(2)}) async-start(), calls=%async_computation | async-start | bytes 33816576 | tf_op jit(solution)/shard_map/all_gather | solution.py:64
  8.5 6.7 %collective-permute-start = (bf16[14,15,256]{2,1,0:T(8,128)(2,1)S(1)}, bf16[14,15,256]{2,1,0:T(8,128)(2,1)S(1)}, u32[]{:S(2)}, u32[]{:S(2)}) collective-permute-start(bf16[14,15,256]{2,1,0:T(8,128)(2,1)S(1)} %slice_bitcast_fusion.9), channel_id=1, source_target_pairs={{0,16},{16,32},{32,48},{48,64},{64,80},{80,96},{96,112},{1,17},{17... | collective-permute-start | bytes 322568 | tf_op jit(solution)/shard_map/ppermute | solution.py:14
  15.2 5.1 %collective-permute-start.1 = (bf16[15,15,256]{2,1,0:T(8,128)(2,1)S(1)}, bf16[15,15,256]{2,1,0:T(8,128)(2,1)S(1)}, u32[]{:S(2)}, u32[]{:S(2)}) collective-permute-start(bf16[15,15,256]{2,1,0:T(8,128)(2,1)S(1)} %fusion.27), channel_id=1, source_target_pairs={{0,1},{1,2},{2,3},{3,4},{4,5},{5,6},{6,7},{7,8},{8,9},{9,10},{10,1... | collective-permute-start | bytes 345608 | tf_op jit(solution)/shard_map/ppermute | solution.py:14
  41.5 2.8 copy-start.3
  78.9 10.2 %copy-start.9 = (f32[15,15,15,256]{3,2,1,0:T(8,128)S(1)}, f32[15,15,15,256]{3,2,1,0:T(8,128)}, u32[]{:S(2)}) copy-start(f32[15,15,15,256]{3,2,1,0:T(8,128)} %reshape.317) | copy-start | bytes 10368004
  80.1 9.1 %slice-start = ((f32[15,15,15,256]{3,2,1,0:T(8,128)}), f32[15,14,15,256]{3,2,1,0:T(8,128)S(1)}, s32[]{:S(2)}) async-start(f32[15,15,15,256]{3,2,1,0:T(8,128)} %reshape.317), calls=%async_computation.1 | async-start | bytes 6881280 | tf_op jit(solution)/shard_map/slice | solution.py:42
  80.1 9.1 %collective-permute-start.2 = (f32[15,15,256]{2,1,0:T(8,128)S(1)}, f32[15,15,256]{2,1,0:T(8,128)S(1)}, u32[]{:S(2)}, u32[]{:S(2)}) collective-permute-start(f32[15,15,256]{2,1,0:T(8,128)S(1)} %slice_bitcast_fusion.2), channel_id=1, source_target_pairs={{1,0},{2,1},{3,2},{4,3},{5,4},{6,5},{7,6},{8,7},{9,8},{10,9},{11,1... | collective-permute-start | bytes 691208 | tf_op jit(solution)/shard_map/ppermute | solution.py:14
  89.2 9.2 %copy-start.8 = (bf16[14,14,13,256]{3,1,2,0:T(8,128)(2,1)S(1)}, bf16[14,14,13,256]{3,1,2,0:T(8,128)(2,1)}, u32[]{:S(2)}) copy-start(bf16[14,14,13,256]{3,1,2,0:T(8,128)(2,1)} %param.17) | copy-start | bytes 3913732
  89.2 9.1 %collective-permute-start.3 = (f32[14,15,256]{2,1,0:T(8,128)S(1)}, f32[14,15,256]{2,1,0:T(8,128)S(1)}, u32[]{:S(2)}, u32[]{:S(2)}) collective-permute-start(f32[14,15,256]{2,1,0:T(8,128)S(1)} %slice_bitcast_fusion.6), channel_id=1, source_target_pairs={{16,0},{32,16},{48,32},{64,48},{80,64},{96,80},{112,96},{17,1},{33... | collective-permute-start | bytes 645128 | tf_op jit(solution)/shard_map/ppermute | solution.py:14
  98.4 1.7 copy-start
  100.1 3.7 collective-permute-start.4
  103.8 6.4 %collective-permute-start.5 = (bf16[15,15,256]{2,1,0:T(8,128)(2,1)S(1)}, bf16[15,15,256]{2,1,0:T(8,128)(2,1)S(1)}, u32[]{:S(2)}, u32[]{:S(2)}) collective-permute-start(bf16[15,15,256]{2,1,0:T(8,128)(2,1)S(1)} %fusion.26), channel_id=1, source_target_pairs={{0,1},{1,2},{2,3},{3,4},{4,5},{5,6},{6,7},{7,8},{8,9},{9,10},{10,1... | collective-permute-start | bytes 345608 | tf_op jit(solution)/shard_map/ppermute | solution.py:14
  131.3 2.8 copy-start.4
  172.3 11.3 %copy-start.10 = (f32[15,15,15,256]{3,2,1,0:T(8,128)S(1)}, f32[15,15,15,256]{3,2,1,0:T(8,128)}, u32[]{:S(2)}) copy-start(f32[15,15,15,256]{3,2,1,0:T(8,128)} %reshape.323) | copy-start | bytes 10368004
  173.5 10.2 %slice-start.1 = ((f32[15,15,15,256]{3,2,1,0:T(8,128)}), f32[15,14,15,256]{3,2,1,0:T(8,128)S(1)}, s32[]{:S(2)}) async-start(f32[15,15,15,256]{3,2,1,0:T(8,128)} %reshape.323), calls=%async_computation.2 | async-start | bytes 6881280 | tf_op jit(solution)/shard_map/slice | solution.py:42
  173.5 10.2 %collective-permute-start.6 = (f32[15,15,256]{2,1,0:T(8,128)S(1)}, f32[15,15,256]{2,1,0:T(8,128)S(1)}, u32[]{:S(2)}, u32[]{:S(2)}) collective-permute-start(f32[15,15,256]{2,1,0:T(8,128)S(1)} %slice_bitcast_fusion.1), channel_id=1, source_target_pairs={{1,0},{2,1},{3,2},{4,3},{5,4},{6,5},{7,6},{8,7},{9,8},{10,9},{11,1... | collective-permute-start | bytes 691208 | tf_op jit(solution)/shard_map/ppermute | solution.py:14
  183.7 7.7 %copy-start.1 = (f32[14,14,15,256]{3,2,1,0:T(8,128)S(1)}, f32[14,14,15,256]{3,2,1,0:T(8,128)}, u32[]{:S(2)}) copy-start(f32[14,14,15,256]{3,2,1,0:T(8,128)} %copy-done) | copy-start | bytes 9031684
  183.7 7.6 %collective-permute-start.7 = (f32[14,15,256]{2,1,0:T(8,128)S(1)}, f32[14,15,256]{2,1,0:T(8,128)S(1)}, u32[]{:S(2)}, u32[]{:S(2)}) collective-permute-start(f32[14,15,256]{2,1,0:T(8,128)S(1)} %slice_bitcast_fusion.5), channel_id=1, source_target_pairs={{16,0},{32,16},{48,32},{64,48},{80,64},{96,80},{112,96},{17,1},{33... | collective-permute-start | bytes 645128 | tf_op jit(solution)/shard_map/ppermute | solution.py:14
  191.4 1.8 copy-start.6
  193.2 3.7 collective-permute-start.8
  196.9 7.1 %collective-permute-start.9 = (bf16[15,15,256]{2,1,0:T(8,128)(2,1)S(1)}, bf16[15,15,256]{2,1,0:T(8,128)(2,1)S(1)}, u32[]{:S(2)}, u32[]{:S(2)}) collective-permute-start(bf16[15,15,256]{2,1,0:T(8,128)(2,1)S(1)} %fusion.25), channel_id=1, source_target_pairs={{0,1},{1,2},{2,3},{3,4},{4,5},{5,6},{6,7},{7,8},{8,9},{9,10},{10,1... | collective-permute-start | bytes 345608 | tf_op jit(solution)/shard_map/ppermute | solution.py:14
  225.1 2.8 copy-start.5
  266.2 11.3 %copy-start.11 = (f32[15,15,15,256]{3,2,1,0:T(8,128)S(1)}, f32[15,15,15,256]{3,2,1,0:T(8,128)}, u32[]{:S(2)}) copy-start(f32[15,15,15,256]{3,2,1,0:T(8,128)} %reshape.329) | copy-start | bytes 10368004
  267.3 10.2 %slice-start.2 = ((f32[15,15,15,256]{3,2,1,0:T(8,128)}), f32[15,14,15,256]{3,2,1,0:T(8,128)S(1)}, s32[]{:S(2)}) async-start(f32[15,15,15,256]{3,2,1,0:T(8,128)} %reshape.329), calls=%async_computation.3 | async-start | bytes 6881280 | tf_op jit(solution)/shard_map/slice | solution.py:42
  267.3 10.2 %collective-permute-start.10 = (f32[15,15,256]{2,1,0:T(8,128)S(1)}, f32[15,15,256]{2,1,0:T(8,128)S(1)}, u32[]{:S(2)}, u32[]{:S(2)}) collective-permute-start(f32[15,15,256]{2,1,0:T(8,128)S(1)} %slice_bitcast_fusion), channel_id=1, source_target_pairs={{1,0},{2,1},{3,2},{4,3},{5,4},{6,5},{7,6},{8,7},{9,8},{10,9},{11,1... | collective-permute-start | bytes 691208 | tf_op jit(solution)/shard_map/ppermute | solution.py:14
  277.6 7.7 %copy-start.2 = (f32[14,14,15,256]{3,2,1,0:T(8,128)S(1)}, f32[14,14,15,256]{3,2,1,0:T(8,128)}, u32[]{:S(2)}) copy-start(f32[14,14,15,256]{3,2,1,0:T(8,128)} %copy-done) | copy-start | bytes 9031684
  277.6 7.7 %copy-start.7 = (f32[14,14,15,256]{3,2,1,0:T(8,128)S(1)}, f32[14,14,15,256]{3,2,1,0:T(8,128)}, u32[]{:S(2)}) copy-start(f32[14,14,15,256]{3,2,1,0:T(8,128)} %copy-done.6) | copy-start | bytes 9031684
  277.6 7.6 %collective-permute-start.11 = (f32[14,15,256]{2,1,0:T(8,128)S(1)}, f32[14,15,256]{2,1,0:T(8,128)S(1)}, u32[]{:S(2)}, u32[]{:S(2)}) collective-permute-start(f32[14,15,256]{2,1,0:T(8,128)S(1)} %slice_bitcast_fusion.4), channel_id=1, source_target_pairs={{16,0},{32,16},{48,32},{64,48},{80,64},{96,80},{112,96},{17,1},{33... | collective-permute-start | bytes 645128 | tf_op jit(solution)/shard_map/ppermute | solution.py:14
  287.6 1.7 copy-start.12
Sparse Core Ops, SparseCore 0:
  295.6 112.2 all-gather.2
